TPU v7x, 512 devices: a whole 4x8x8 slice. The times are simulated.
512 devices in a mesh: dom: 32 (over y, x), orient: 16 (over z, core).
Axes of the slice: x: 4, y: 8, z: 8, core: 2. Of those that a mesh axis runs over, the one named last changes fastest.
Arguments:
- particles: bfloat16 [256, 2, 8192], P('dom'), may hold values from -4 to 4
- references: bfloat16 [256, 2, 8192], P('orient'), may hold values from -1.7 to 1.7
- phases: float32 [16, 8192], replicated, may hold values from -3.1416 to 3.1416
- mask: int32 [256, 256], P('dom', 'orient'), may hold values from 0 to 1, as said below
- ctf_group: int32 [256], replicated, may hold values from 0 to 63
- ctf_table: float32 [64, 64], replicated, may hold values from 0.1 to 1
- shell_index: int32 [8192], replicated, may hold values from 0 to 63
- sigma2: float32 [64], replicated, may hold values from 8 to 32
Outputs:
- posterior: float32 [256, 16, 256], P('dom', None, 'orient')
- image_sums: float32 [256, 2, 8192], P('orient', None, 'dom')
- ctf_weights: float32 [256, 64], P('orient')
- shell_noise: float32 [64], replicated
Inputs may be any that keep to these rules, and one draw needn't show every extreme that they name: `mask`: every particle allows at least one orientation.
All inputs are finite; a program needn't handle non-finite values.
Results may differ from a plain program's by a relative error of at most 0.0041.
Values may be sent and summed in bfloat16 or wider, within the bound.
A program may use at most 192 MiB of HBM per device.

v0:
```python
import jax
import jax.numpy as jnp
from jax import lax
from jax.sharding import PartitionSpec as P

trans_block = 2


def make_images(planes, ctf_pix, cosine, sine_part):
    real_part = planes[:, 0][:, None, :]
    imag_part = planes[:, 1][:, None, :]
    shifted_real = real_part * cosine[None] - imag_part * sine_part[None]
    shifted_imag = real_part * sine_part[None] + imag_part * cosine[None]
    factor = ctf_pix[:, None, :]
    return jnp.stack([factor * shifted_real, factor * shifted_imag], axis=2).astype(jnp.bfloat16)


def on_device(particles, references, phases, mask, ctf_group, ctf_table, shell_index, sigma2):
    highest = lax.Precision.HIGHEST
    part_dev = particles.shape[0]
    ori_dev = references.shape[0]
    pixels = shell_index.shape[0]
    shells = ctf_table.shape[1]
    trans_count = phases.shape[0]
    blocks = trans_count // trans_block
    dom_size = lax.axis_size("dom")
    width = pixels // dom_size
    dom_index = lax.axis_index("dom")
    shell_pick = (shell_index[:, None] == jnp.arange(shells, dtype=jnp.int32)[None, :]).astype(
        jnp.float32
    )
    group_pick = (
        ctf_group[:, None] == jnp.arange(ctf_table.shape[0], dtype=jnp.int32)[None, :]
    ).astype(jnp.float32)
    ctf_all = jnp.dot(group_pick, ctf_table, precision=highest)
    ctf_rows = lax.dynamic_slice_in_dim(ctf_all, dom_index * part_dev, part_dev, 0)
    ctf_pix = jnp.dot(ctf_rows, shell_pick.T, precision=highest)
    sigma_pix = jnp.dot(shell_pick, sigma2, precision=highest)
    refs_wide = references.astype(jnp.float32)
    weighted = (refs_wide / sigma_pix).astype(jnp.bfloat16)
    ref_norm = jnp.dot(jnp.sum(refs_wide * refs_wide, axis=1), shell_pick, precision=highest)
    energy = ref_norm / sigma2
    ctf_square = ctf_rows * ctf_rows
    quadratic = 0.5 * jnp.dot(ctf_square, energy.T, precision=highest)
    planes = particles.astype(jnp.float32)
    cosines = jnp.cos(phases)
    sine_rows = jnp.sin(phases)

    def score_block(index):
        first = index * trans_block
        images = make_images(
            planes,
            ctf_pix,
            lax.dynamic_slice_in_dim(cosines, first, trans_block, 0),
            lax.dynamic_slice_in_dim(sine_rows, first, trans_block, 0),
        )
        cross = jnp.einsum("ptcx,ocx->pto", images, weighted, preferred_element_type=jnp.float32)
        return cross - quadratic[:, None, :]

    stacked = lax.map(score_block, jnp.arange(blocks, dtype=jnp.int32))
    scores = jnp.moveaxis(stacked, 0, 1).reshape(part_dev, trans_count, ori_dev)
    scores = jnp.where((mask == 1)[:, None, :], scores, -1e30)
    local_peak = jnp.max(scores, axis=(1, 2))
    peak = lax.pmax(local_peak, "orient")
    total = lax.psum(jnp.sum(jnp.exp(scores - peak[:, None, None]), axis=(1, 2)), "orient")
    posterior = jnp.exp(scores - peak[:, None, None]) / total[:, None, None]
    post_half = posterior.astype(jnp.bfloat16)
    weight_rows = jnp.sum(posterior, axis=1)
    ctf_part = jnp.dot(weight_rows.T, ctf_square, precision=highest)
    part_norm = jnp.dot(jnp.sum(planes * planes, axis=1), shell_pick, precision=highest)
    term_one = jnp.sum(part_norm * jnp.sum(weight_rows, axis=1)[:, None], axis=0)
    term_three = jnp.sum(ctf_part * ref_norm, axis=0)
    start_pix = dom_index * width
    pick_cols = lax.dynamic_slice_in_dim(shell_pick, start_pix, width, 0)

    def add_block(index, running):
        first = index * trans_block
        images = make_images(
            planes,
            ctf_pix,
            lax.dynamic_slice_in_dim(cosines, first, trans_block, 0),
            lax.dynamic_slice_in_dim(sine_rows, first, trans_block, 0),
        )
        weights = lax.dynamic_slice_in_dim(post_half, first, trans_block, 1)
        return running + jnp.einsum(
            "pto,ptcx->ocx", weights, images, preferred_element_type=jnp.float32
        )

    partial_sums = lax.fori_loop(0, blocks, add_block, jnp.zeros((ori_dev, 2, pixels), jnp.float32))
    image_sums = lax.psum_scatter(partial_sums, "dom", scatter_dimension=2, tiled=True)
    ref_cols = lax.dynamic_slice_in_dim(refs_wide, start_pix, width, 2)
    term_two = -2.0 * jnp.dot(
        jnp.sum(image_sums * ref_cols, axis=(0, 1)), pick_cols, precision=highest
    )
    ctf_weights = lax.psum(ctf_part, "dom")
    shell_total = lax.psum(term_one + term_two + term_three, ("dom", "orient"))
    divisor = part_dev * dom_size * pixels / shells
    return (posterior, image_sums, ctf_weights, shell_total / divisor)


def solution(mesh):
    return jax.shard_map(
        on_device,
        mesh=mesh,
        in_specs=(
            P("dom", None, None),
            P("orient", None, None),
            P(),
            P("dom", "orient"),
            P(),
            P(),
            P(),
            P(),
        ),
        out_specs=(P("dom", None, "orient"), P("orient", None, "dom"), P("orient", None), P()),
        check_vma=False,
    )
```

profile of v0, /device:TPU:1, one launch (start us, length us, event | category | flops | bytes accessed | tf_op | source)
XLA Modules:
  0.0 511.5 jit_solution(465495128250471743)
XLA Ops:
  7.3 0.7 broadcast_compare_fusion
  8.0 1.1 copy_convert_fusion
  9.1 2.8 fusion.46
  12.0 0.7 fusion.15
  12.7 1.9 multiply_reduce_fusion
  14.6 1.1 copy.23
  15.7 1.1 fusion.14
  17.1 0.7 fusion.16
  18.0 21.1 %while.24 = (s32[]{:T(128)}, f32[8,8,2,16]{3,1,2,0:T(8,128)S(1)}, f32[8,8192]{1,0:T(8,128)S(1)}, f32[8,2,8192]{2,0,1:T(8,128)S(1)}, s32[8]{0:T(128)S(1)}, /*inde...) while((s32[]{:T(128)}, f32[8,8,2,16]{3,1,2,0:T(8,128)S(1)}, ...), condition=%wide.region_2.3_spmd, body=%wide.region_1.2_spmd.sunk | while | flops 9961734 | bytes 5910755 | solution.py:60
  19.5 0.8 copy-done.4
  22.2 0.8 copy-done.4
  24.8 0.8 copy-done.4
  27.4 0.8 copy-done.4
  30.1 0.8 copy-done.4
  32.7 0.8 copy-done.4
  35.3 0.8 copy-done.4
  38.0 0.8 copy-done.4
  39.2 30.6 %pmax.7 = f32[8]{0:T(128)S(1)} all-reduce(f32[8]{0:T(128)S(1)} %select_reduce_fusion), channel_id=1, replica_groups=mesh['dom'=32,'orient'=16] {'orient'}, use_global_device_ids=true, to_apply=%region_4.5 | all-reduce | flops 8 | bytes 64 | tf_op jit(solution)/shard_map/pmax | solution.py:64
  70.0 25.8 %psum.21 = f32[8]{0:T(128)S(1)} all-reduce(f32[8]{0:T(128)S(1)} %fusion.30), channel_id=1, replica_groups=mesh['dom'=32,'orient'=16] {'orient'}, use_global_device_ids=true, to_apply=%region_6.7 | all-reduce | flops 8 | bytes 64 | tf_op jit(solution)/shard_map/psum | solution.py:65
  95.9 0.7 fusion.45
  96.6 6.0 %while.25 = (s32[]{:T(128)}, f32[16,2,8192]{2,0,1:T(8,128)S(1)}, bf16[8,16,16]{2,1,0:T(8,128)(2,1)S(1)}, f32[8,8192]{1,0:T(8,128)S(1)}, f32[8,2,8192]{2,0,1:T(8,...) while((s32[]{:T(128)}, f32[16,2,8192]{2,0,1:T(8,128)S(1)}, ...), condition=%wide.region_8.9_spmd.clone, body=%wide.region_7.8_spmd.clone.sunk | while | flops 11272199 | bytes 5375669 | solution.py:89
  102.6 31.4 %copy.29 = f32[16,2,8192]{1,0,2:T(8,128)} copy(f32[16,2,8192]{2,0,1:T(8,128)S(1)} %get-tuple-element.176) | data formatting | bytes 2097152
  134.0 46.1 %reshape.85 = f32[8192,32]{1,0:T(8,128)} reshape(f32[8192,16,2]{2,1,0:T(8,128)} %bitcast.18) | data formatting | bytes 2097152
  181.0 0.9 multiply_reduce_fusion.3
  182.3 63.1 %psum.22 = f32[16,64]{1,0:T(8,128)} all-reduce(f32[16,64]{1,0:T(8,128)S(1)} %get-tuple-element.302), channel_id=1, replica_groups=mesh['dom'=32,'orient'=16] {'dom'}, use_global_device_ids=true, to_apply=%region_11.12 | all-reduce | flops 1024 | bytes 8192 | tf_op jit(solution)/shard_map/psum | solution.py:95
  245.5 1.1 fusion.18
  246.6 1.1 iota_compare_fusion
  247.7 150.6 %reduce-scatter.4.cloned.1.call-done = f32[256,32]{1,0:T(8,128)} async-done(((f32[8192,32]{1,0:T(8,128)}), f32[256,32]{1,0:T(8,128)}) %reduce-scatter.4.cloned.1.call-update) | async-done | bytes 32784
  398.3 2.1 reshape.86
  400.5 1.0 copy.30
  401.6 0.8 fusion.21
  402.4 101.8 %psum.23 = f32[64]{0:T(128)S(1)} all-reduce(f32[64]{0:T(128)S(1)} %fusion.21), channel_id=1, replica_groups=mesh['dom'=32,'orient'=16] {'dom','orient'}, use_global_device_ids=true, to_apply=%region_17.18 | all-reduce | flops 64 | bytes 512 | tf_op jit(solution)/shard_map/psum | solution.py:96
  (127 shorter events, 17.8 us)
Async XLA Ops:
  7.2 9.6 %copy-start = (f32[64,64]{1,0:T(8,128)S(1)}, f32[64,64]{1,0:T(8,128)}, u32[]{:S(2)}) copy-start(f32[64,64]{1,0:T(8,128)} %param.17) | copy-start | bytes 49156
  7.2 4.7 copy-start.7
  7.2 4.7 copy-start.12
  7.2 5.5 %copy-start.1 = (bf16[16,2,8192]{2,1,0:T(2,128)(2,1)S(1)}, bf16[16,2,8192]{2,1,0:T(2,128)(2,1)}, u32[]{:S(2)}) copy-start(bf16[16,2,8192]{2,1,0:T(2,128)(2,1)} %param.13) | copy-start | bytes 1572868
  7.2 391.1 %reduce-scatter.4.cloned.1.call-start = ((), (), s32[]{:S(2)}) async-start(), calls=%async_computation.1 | async-start | bytes 4325376
  11.9 4.9 copy-start.11
  17.1 0.9 copy-start.5
  19.2 1.0 copy-start.4
  21.9 1.0 copy-start.4
  24.5 1.0 copy-start.4
  27.2 1.0 copy-start.4
  29.8 1.0 copy-start.4
  32.4 1.0 copy-start.4
  35.0 1.0 copy-start.4
  37.7 1.0 copy-start.4
  95.8 0.8 copy-start.9
  180.1 0.7 copy-start.10
  180.1 1.8 copy-start.2
  180.1 65.3 %copy-start.3 = (bf16[8,2,8192]{2,1,0:T(2,128)(2,1)S(1)}, bf16[8,2,8192]{2,1,0:T(2,128)(2,1)}, u32[]{:S(2)}) copy-start(bf16[8,2,8192]{2,1,0:T(2,128)(2,1)} %param.12) | copy-start | bytes 786436
  180.8 64.8 %copy-start.8 = (s32[8192]{0:T(1024)S(1)}, s32[8192]{0:T(1024)}, u32[]{:S(2)}) copy-start(s32[8192]{0:T(1024)} %param.18) | copy-start | bytes 98308
  401.5 103.2 %copy-start.6 = (f32[16,2,256]{2,1,0:T(2,128)}, f32[16,2,256]{2,1,0:T(2,128)S(1)}, u32[]{:S(2)}) copy-start(f32[16,2,256]{2,1,0:T(2,128)S(1)} %copy.30) | copy-start | bytes 98308
Sparse Core Ops, SparseCore 0:
  180.3 218.0 reduce-scatter.3
where the time goes:
time: 513 us; the launch traced here: 512 us
  blocking collectives  221 us (43%)
  waiting for transfers between devices  151 us (29%)
  local copies, waits for them, and re-layouts  97.7 us (19%)
  between operations  14.2 us (3%)
  matrix products  11.8 us (2%)
  other arithmetic  9.8 us (2%)
  loops' own time  6.02 us (1%)
    unnamed x2, waiting for transfers between devices  151 us
    psum x1, blocking collectives, on_device(): shell_total = lax.psum(term_one + term_two + term_three, ('dom', 'orient'))  102 us
    unnamed x28, local copies, waits for them, and re-layouts  81.4 us
    psum x1, blocking collectives, on_device(): ctf_weights = lax.psum(ctf_part, 'dom')  63.1 us
    pmax x1, blocking collectives, on_device(): peak = lax.pmax(local_peak, 'orient')  30.6 us
    psum x1, blocking collectives, on_device(): lax.psum(jnp.sum(jnp.exp(scores - peak[:, None, None]), axis=(1, 2)), 'or...  25.8 us
  transfers between devices with their start and end apart: 1, of which 1 were waited for; matrix products, arithmetic and copies ran while one was open for 1% of the time, Pallas kernels for 0%

commit v1 on v0

--- a/solution.py
+++ b/solution.py
@@ -4,6 +4,12 @@
 from jax.sharding import PartitionSpec as P
 
 trans_block = 2
+
+
+def gather_and_add(value, axis):
+    parts = lax.all_gather(value, axis, axis=0, tiled=False)
+    result = parts.sum(axis=0)
+    return result
 
 
 def make_images(planes, ctf_pix, cosine, sine_part):
@@ -93,7 +99,7 @@
         jnp.sum(image_sums * ref_cols, axis=(0, 1)), pick_cols, precision=highest
     )
     ctf_weights = lax.psum(ctf_part, "dom")
-    shell_total = lax.psum(term_one + term_two + term_three, ("dom", "orient"))
+    shell_total = gather_and_add(term_one + term_two + term_three, ("dom", "orient"))
     divisor = part_dev * dom_size * pixels / shells
     return (posterior, image_sums, ctf_weights, shell_total / divisor)
 

time: 513 us -> 680 us (1.33)
  waiting for transfers between devices: 151 us -> 420 us
  blocking collectives: 221 us -> 116 us
    unnamed x2 -> x4, waiting for transfers between devices: 151 us -> 420 us
    psum x1 -> x0, blocking collectives: 102 us -> none  [on_device(): shell_total = lax.psum(term_one + term_two + term_three, ('dom', 'orient'))]
    unnamed x28 -> x32, local copies, waits for them, and re-layouts: 81.4 us -> 82.2 us
  transfers between devices with their start and end apart: 1 -> 2, of which waited for: 1 -> 2; matrix products, arithmetic and copies ran while one was open for 1% -> 1% of each run, Pallas kernels for 0% -> 0%
where the time goes in v1:
time: 680 us; the launch traced here: 678 us
  waiting for transfers between devices  420 us (62%)
  blocking collectives  116 us (17%)
  local copies, waits for them, and re-layouts  99.6 us (15%)
  between operations  14.3 us (2%)
  matrix products  11.8 us (2%)
  other arithmetic  9.89 us (1%)
    unnamed x4, waiting for transfers between devices  420 us
    unnamed x32, local copies, waits for them, and re-layouts  82.2 us
    psum x1, blocking collectives, on_device(): ctf_weights = lax.psum(ctf_part, 'dom')  60 us
    pmax x1, blocking collectives, on_device(): peak = lax.pmax(local_peak, 'orient')  30.6 us
    psum x1, blocking collectives, on_device(): lax.psum(jnp.sum(jnp.exp(scores - peak[:, None, None]), axis=(1, 2)), 'or...  25.8 us
  transfers between devices with their start and end apart: 2, of which 2 were waited for; matrix products, arithmetic and copies ran while one was open for 1% of the time, Pallas kernels for 0%

profile of v1, /device:TPU:1, one launch (start us, length us, event | category | flops | bytes accessed | tf_op | source)
XLA Modules:
  0.0 678.0 jit_solution(8481381124698453216)
XLA Ops:
  7.3 0.7 broadcast_compare_fusion
  8.0 1.1 copy_convert_fusion
  9.1 2.8 fusion.46
  12.0 0.7 fusion.15
  12.7 1.9 multiply_reduce_fusion
  14.6 1.1 copy.28
  15.7 1.1 fusion.14
  17.1 0.7 fusion.16
  18.0 21.1 %while.24 = (s32[]{:T(128)}, f32[8,8,2,16]{3,1,2,0:T(8,128)S(1)}, f32[8,8192]{1,0:T(8,128)S(1)}, f32[8,2,8192]{2,0,1:T(8,128)S(1)}, s32[8]{0:T(128)S(1)}, /*inde...) while((s32[]{:T(128)}, f32[8,8,2,16]{3,1,2,0:T(8,128)S(1)}, ...), condition=%wide.region_2.3_spmd, body=%wide.region_1.2_spmd.sunk | while | flops 9961734 | bytes 5910755 | solution.py:66
  19.5 0.8 copy-done.4
  22.2 0.8 copy-done.4
  24.8 0.8 copy-done.4
  27.4 0.8 copy-done.4
  30.1 0.8 copy-done.4
  32.7 0.8 copy-done.4
  35.3 0.8 copy-done.4
  38.0 0.8 copy-done.4
  39.2 30.6 %pmax.7 = f32[8]{0:T(128)S(1)} all-reduce(f32[8]{0:T(128)S(1)} %select_reduce_fusion), channel_id=1, replica_groups=mesh['dom'=32,'orient'=16] {'orient'}, use_global_device_ids=true, to_apply=%region_4.5 | all-reduce | flops 8 | bytes 64 | tf_op jit(solution)/shard_map/pmax | solution.py:70
  70.0 25.8 %psum.14 = f32[8]{0:T(128)S(1)} all-reduce(f32[8]{0:T(128)S(1)} %fusion.30), channel_id=1, replica_groups=mesh['dom'=32,'orient'=16] {'orient'}, use_global_device_ids=true, to_apply=%region_6.7 | all-reduce | flops 8 | bytes 64 | tf_op jit(solution)/shard_map/psum | solution.py:71
  96.6 6.0 while.25
  102.6 31.4 %copy.34 = f32[16,2,8192]{1,0,2:T(8,128)} copy(f32[16,2,8192]{2,0,1:T(8,128)S(1)} %get-tuple-element.176) | data formatting | bytes 2097152
  134.0 46.1 %reshape.88 = f32[8192,32]{1,0:T(8,128)} reshape(f32[8192,16,2]{2,1,0:T(8,128)} %bitcast.18) | data formatting | bytes 2097152
  181.2 1.1 fusion.18
  182.8 0.9 multiply_reduce_fusion.3
  183.7 1.1 iota_compare_fusion
  184.7 213.3 %reduce-scatter.4.cloned.1.call-done = f32[256,32]{1,0:T(8,128)} async-done(((f32[8192,32]{1,0:T(8,128)}), f32[256,32]{1,0:T(8,128)}) %reduce-scatter.4.cloned.1.call-update) | async-done | bytes 32784
  398.1 2.1 reshape.89
  400.2 1.0 copy.35
  401.3 0.8 fusion.21
  403.2 60.0 %psum.15 = f32[16,64]{1,0:T(8,128)} all-reduce(f32[16,64]{1,0:T(8,128)S(1)} %get-tuple-element.318), channel_id=1, replica_groups=mesh['dom'=32,'orient'=16] {'dom'}, use_global_device_ids=true, to_apply=%region_11.12 | all-reduce | flops 1024 | bytes 8192 | tf_op jit(solution)/shard_map/psum | solution.py:101
  463.2 206.4 %all-reduce.3.cloned.1.call-done = f32[32768]{0:T(1024)} async-done(((f32[32768]{0:T(1024)}), f32[32768]{0:T(1024)}) %all-reduce.3.cloned.1.call-update) | async-done | bytes 131088
  669.6 1.0 reshape.77
  (135 shorter events, 19.7 us)
Async XLA Ops:
  7.2 9.6 %copy-start = (f32[64,64]{1,0:T(8,128)S(1)}, f32[64,64]{1,0:T(8,128)}, u32[]{:S(2)}) copy-start(f32[64,64]{1,0:T(8,128)} %param.17) | copy-start | bytes 49156
  7.2 4.7 copy-start.8
  7.2 4.7 copy-start.13
  7.2 5.5 copy-start.1
  7.2 390.9 %reduce-scatter.4.cloned.1.call-start = ((), (), s32[]{:S(2)}) async-start(), calls=%async_computation.2 | async-start | bytes 4325376
  11.9 4.9 copy-start.12
  17.1 0.9 copy-start.6
  19.2 1.0 copy-start.4
  21.9 1.0 copy-start.4
  24.5 1.0 copy-start.4
  27.2 1.0 copy-start.4
  29.8 1.0 copy-start.4
  32.4 1.0 copy-start.4
  35.0 1.0 copy-start.4
  37.7 1.0 copy-start.4
  95.8 0.8 copy-start.10
  180.1 0.7 copy-start.11
  180.1 1.0 copy-start.3
  180.1 1.1 copy-start.9
  180.1 2.2 copy-start.2
  180.2 489.4 %all-reduce.3.cloned.1.call-start = ((), (), s32[]{:S(2)}) async-start(), calls=%async_computation.1 | async-start | bytes 262144
  401.3 269.9 %copy-start.7 = (f32[16,2,256]{2,1,0:T(2,128)}, f32[16,2,256]{2,1,0:T(2,128)S(1)}, u32[]{:S(2)}) copy-start(f32[16,2,256]{2,1,0:T(2,128)S(1)} %copy.35) | copy-start | bytes 98308
  402.5 0.7 copy-start.5
Sparse Core Ops, SparseCore 0:
  180.3 217.7 reduce-scatter.3
  403.8 265.7 all-reduce.2
